TPU v7x, 256 devices: a whole 4x4x8 slice. The times are simulated.
256 devices in a mesh: mod: 2 (over core), seq: 8 (over z), tp: 16 (over x, y).
Axes of the slice: x: 4, y: 4, z: 8, core: 2. Of those that a mesh axis runs over, the one named last changes fastest.
Arguments:
- tokens: bfloat16 [8192, 4096], P(('mod', 'seq'), 'tp'), may hold values from -6 to 6
- modality: int32 [8192], replicated, may hold values from 0 to 1, as said below
- norm_gain: float32 [2, 4096], replicated, may hold values from 0.1 to 1.9
- input_weight: bfloat16 [2, 4096, 3, 4096], P('mod', None, None, 'tp'), may hold values from -0.09375 to 0.09375
- head_gain: float32 [2, 2, 128], replicated, may hold values from 1 to 2
- output_weight: bfloat16 [2, 4096, 4096], P('mod', 'tp'), may hold values from -0.125 to 0.125
Outputs:
- update: bfloat16 [8192, 4096], P(('mod', 'seq'), 'tp')
Inputs may be any that keep to these rules, and one draw needn't show every extreme that they name: Each value is constant over aligned spans of 64 tokens. Each token shard (the 512 tokens of one index of mod+seq) holds between 3 and 5 image spans, so at most 320 tokens of either modality. In every draw, for some index of seq both of its token shards hold 320 text tokens, and for another index of seq both hold 320 image tokens.
All inputs are finite; a program needn't handle non-finite values.
Results may differ from a plain program's by a relative error of at most 0.019.
Values may be sent and summed in bfloat16 or wider, within the bound.
A program may use at most 192 MiB of HBM per device.

v0:
```python
from functools import partial
import math

import jax
import jax.numpy as jnp
from jax import lax
from jax.sharding import PartitionSpec as P

HD = 128
CAP = 320


epsilon = 1e-05
sentinel = 1 << 30


def route_table(shard_ids, shard_index, slot_count):
    length = shard_ids.shape[0]
    order = jnp.argsort(shard_ids, stable=True)
    text_count = jnp.sum((shard_ids == 0).astype(jnp.int32))
    padded = jnp.concatenate([order, jnp.zeros((slot_count,), jnp.int32)])
    slot_index = jnp.arange(slot_count, dtype=jnp.int32)
    picked = jnp.stack(
        [padded[:slot_count], lax.dynamic_slice_in_dim(padded, text_count, slot_count)]
    )
    live = jnp.stack([slot_index < text_count, slot_index < length - text_count])
    place = shard_index * length + picked
    query_place = jnp.where(live, place, -1)
    key_place = jnp.where(live, place, sentinel)
    return (order, text_count, picked, live, query_place, key_place)


def select_rows(table, picked, live):
    return jnp.where(live[:, :, None], table[picked], jnp.zeros((), table.dtype))


def head_norm(part, gain):
    return part * lax.rsqrt(jnp.mean(part * part, axis=-1, keepdims=True) + epsilon) * gain


def body(tokens, modality, norm_gain, input_weight, head_gain, output_weight):
    length = tokens.shape[0]
    mod_count = lax.axis_size("mod")
    seq_count = lax.axis_size("seq")
    shards = mod_count * seq_count
    mine = lax.axis_index("mod")
    seq_index = lax.axis_index("seq")
    all_ids = modality.reshape(shards, length)
    own_index = mine * seq_count + seq_index
    own_ids = lax.dynamic_index_in_dim(all_ids, own_index, 0, keepdims=False)
    own_table = route_table(own_ids, own_index, CAP)
    order = own_table[0]
    text_count = own_table[1]
    picked = own_table[2]
    live = own_table[3]
    tables = jax.vmap(partial(route_table, slot_count=CAP))(
        all_ids, jnp.arange(shards, dtype=jnp.int32)
    )
    query_grid = tables[4].reshape(mod_count, seq_count, 2, CAP)
    own_query = lax.dynamic_index_in_dim(query_grid, seq_index, 1, keepdims=False)
    own_query = lax.dynamic_index_in_dim(own_query, mine, 1, keepdims=False).reshape(
        mod_count * CAP
    )
    key_grid = tables[5].reshape(mod_count, seq_count, 2, CAP)
    key_order = jnp.transpose(key_grid, (2, 1, 0, 3)).reshape(shards * mod_count * CAP)
    gathered = lax.all_gather(tokens, "tp", axis=1, tiled=True)
    arrived = lax.all_to_all(
        select_rows(gathered, picked, live), "mod", split_axis=0, concat_axis=0, tiled=True
    )
    rows_total = arrived.shape[0] * arrived.shape[1]
    width = arrived.shape[2]
    states = arrived.reshape(rows_total, width).astype(jnp.float32)
    gain = lax.dynamic_index_in_dim(norm_gain, mine, 0, keepdims=False)
    normed = (
        states * lax.rsqrt(jnp.mean(states * states, axis=1, keepdims=True) + epsilon) * gain
    ).astype(jnp.bfloat16)
    local_width = input_weight.shape[3]
    heads_here = local_width // HD
    projected = jnp.dot(
        normed, input_weight[0].reshape(width, 3 * local_width), preferred_element_type=jnp.float32
    )
    projected = projected.reshape(rows_total, 3, heads_here, HD)
    gains = lax.dynamic_index_in_dim(head_gain, mine, 0, keepdims=False)
    query_rows = head_norm(projected[:, 0], gains[0]).astype(jnp.bfloat16)
    key_rows = (
        head_norm(projected[:, 1], gains[1]).astype(jnp.bfloat16).reshape(rows_total, local_width)
    )
    value_rows = projected[:, 2].astype(jnp.bfloat16).reshape(rows_total, local_width)
    scale = 1.0 / math.sqrt(HD)
    key_piece = lax.all_gather(key_rows, ("mod", "seq"), axis=0, tiled=True)
    value_piece = lax.all_gather(value_rows, ("mod", "seq"), axis=0, tiled=True)
    count = key_piece.shape[0]
    scores = (
        jnp.einsum(
            "rhe,khe->hrk",
            query_rows,
            key_piece.reshape(count, heads_here, HD),
            preferred_element_type=jnp.float32,
        )
        * scale
    )
    weights = jnp.where(key_order[None, None, :] <= own_query[None, :, None], jnp.exp(scores), 0.0)
    totals = jnp.sum(weights, axis=2)
    rounded = weights.astype(jnp.bfloat16)
    weighted = jnp.einsum(
        "hrk,khe->rhe",
        rounded,
        value_piece.reshape(count, heads_here, HD),
        preferred_element_type=jnp.float32,
    )
    weighted, totals = (weighted, totals)
    totals = jnp.where(own_query[None, :] >= 0, totals, 1.0)
    attention = (
        (weighted / jnp.transpose(totals)[:, :, None])
        .astype(jnp.bfloat16)
        .reshape(rows_total, local_width)
    )
    head_terms = jnp.dot(attention, output_weight[0], preferred_element_type=jnp.float32)
    summed = lax.psum_scatter(
        head_terms.astype(jnp.bfloat16), "tp", scatter_dimension=1, tiled=True
    ).astype(jnp.float32)
    result = summed.astype(jnp.bfloat16).reshape(mod_count, CAP, summed.shape[1])
    returned = lax.all_to_all(result, "mod", split_axis=0, concat_axis=0, tiled=True)
    flat = returned.reshape(mod_count * CAP, summed.shape[1])
    inverse = jnp.zeros((length,), jnp.int32).at[order].set(jnp.arange(length, dtype=jnp.int32))
    slot = own_ids * CAP + inverse - own_ids * text_count
    return flat[slot]


def solution(mesh):
    in_specs = (
        P(("mod", "seq"), "tp"),
        P(),
        P(),
        P("mod", None, None, "tp"),
        P(),
        P("mod", "tp", None),
    )
    out_specs = P(("mod", "seq"), "tp")
    return jax.shard_map(body, mesh=mesh, in_specs=in_specs, out_specs=out_specs, check_vma=False)
```

profile of v0, /device:TPU:1, one launch (start us, length us, event | category | flops | bytes accessed | tf_op | source)
XLA Modules:
  0.0 324.6 jit_solution(6976612528921012147)
XLA Ops:
  7.4 0.7 all-gather.4.cloned.1.call-update
  8.1 1.4 reshape.304
  9.5 0.6 broadcast_in_dim.70
  10.2 0.7 constant_dynamic-slice_fusion.3
  10.9 0.7 convert_reduce_fusion.1
  12.9 3.8 %sort.34 = (s32[512]{0:T(512)}, s32[512]{0:T(512)S(1)}) sort(s32[512]{0:T(512)S(1)} %bitcast.92, s32[512]{0:T(512)S(1)} %iota.35), dimensions={0}, to_apply=%region_1.2 | sort | flops 4608 | bytes 8192 | tf_op jit(solution)/shard_map/jit(argsort)/sort | solution.py:19
  18.2 0.6 iota_compare_fusion.2
  18.8 8.8 %copy.12 = bf16[1,4096,3,256]{1,3,2,0:T(8,128)(2,1)} copy(bf16[1,4096,3,256]{3,1,2,0:T(8,128)(2,1)} %param.9) | data formatting | bytes 12582912 | tf_op args[3]
  27.7 48.4 %all-gather.4.cloned.1.call-done = bf16[512,4096]{1,0:T(8,128)(2,1)} async-done(((bf16[512,256]{1,0:T(8,128)(2,1)}), bf16[512,4096]{1,0:T(8,128)(2,1)}) %all-gather.4.cloned.1.call-update) | async-done | bytes 4194320 | tf_op jit(solution)/shard_map/all_gather | solution.py:66
  76.1 14.3 %gather_fusion = bf16[640,4096]{1,0:T(8,128)(2,1)} fusion(bf16[512,4096]{1,0:T(8,128)(2,1)} %all-gather.4.cloned.1.call-done, s32[1024]{0:T(1024)S(1)} %pad_clamp_fusion.1), kind=kCustom, calls=%fused_computation | custom fusion | bytes 10488320 | tf_op jit(solution)/shard_map/gather | solution.py:34
  90.5 2.9 broadcast_select_fusion
  93.4 9.2 %all_to_all.10 = bf16[2,320,4096]{2,1,0:T(8,128)(2,1)S(1)} all-to-all(bf16[2,320,4096]{2,1,0:T(8,128)(2,1)S(1)} %broadcast_select_fusion), channel_id=1, replica_groups=mesh['mod'=2,'seq'=8,'tp'=16] {'mod'}, dimensions={0} | all-to-all | bytes 10485760 | tf_op jit(solution)/shard_map/all_to_all | solution.py:67
  102.6 1.1 fusion.5
  103.7 2.1 fusion.7
  105.8 5.1 %fusion.29 = f32[640,3,2,128]{0,3,2,1:T(8,128)S(1)} fusion(bf16[640,4096,1,1]{1,0,3,2:T(8,128)(2,1)S(1)} %bitcast.85, bf16[3,2,128,4096]{3,2,1,0:T(8,128)(2,1)S(1)} %bitcast.84), kind=kOutput, calls=%fused_computation.75 | convolution fusion | flops 4026531840 | bytes 13500416 | tf_op jit(solution)/shard_map/dot_general | solution.py:79
  110.9 1.3 copy-done.1
  112.3 0.8 fusion.19
  113.5 0.8 concatenate.26
  114.3 0.7 slice_bitcast_fusion.1
  115.0 1.8 slice.59
  117.2 30.9 %while.1 = (s32[]{:T(128)}, s32[16,832]{1,0:T(8,128)S(1)}, s32[16,2]{0,1:T(2,128)S(1)}, s32[16,320]{1,0:T(8,128)S(1)}, s32[]{:T(128)}, /*index=5*/s32[]{:T(128)}) while((s32[]{:T(128)}, s32[16,832]{1,0:T(8,128)S(1)}, s32[16,2]{0,1:T(2,128)S(1)}, s32[16,320]{1,0:T(8,128)S(1)}, s32[]{:T(128)}, /*index=5*/s32[]{:T(128)}) %tuple.26), condition=%wide.while_cond, body=%wide.while_body.sunk | while | flops 2 | bytes 5233 | solution.py:24
  117.3 0.5 fusion.36
  117.8 1.3 dynamic-slice.9
  119.2 0.5 fusion.36
  119.7 1.3 dynamic-slice.9
  121.1 0.5 fusion.36
  121.6 1.3 dynamic-slice.9
  123.0 0.5 fusion.36
  123.6 1.3 dynamic-slice.9
  125.0 0.5 fusion.36
  125.5 1.3 dynamic-slice.9
  126.9 0.5 fusion.36
  127.4 1.3 dynamic-slice.9
  128.8 0.5 fusion.36
  129.4 1.3 dynamic-slice.9
  130.8 0.5 fusion.36
  131.3 1.3 dynamic-slice.9
  132.7 0.5 fusion.36
  133.2 1.3 dynamic-slice.9
  134.6 0.5 fusion.36
  135.2 1.3 dynamic-slice.9
  136.6 0.5 fusion.36
  137.1 1.3 dynamic-slice.9
  138.5 0.5 fusion.36
  139.0 1.3 dynamic-slice.9
  140.4 0.5 fusion.36
  140.9 1.3 dynamic-slice.9
  142.3 0.5 fusion.36
  142.9 1.3 dynamic-slice.9
  144.3 0.5 fusion.36
  144.8 1.3 dynamic-slice.9
  146.2 0.5 fusion.36
  146.7 1.3 dynamic-slice.9
  148.4 6.8 %broadcast_compare_fusion = pred[640,10240]{1,0:T(8,128)(4,1)} fusion(s32[10240]{0:T(1024)S(1)} %le.22, s32[640]{0:T(1024)S(1)} %le.24), kind=kLoop, calls=%fused_computation.9 | loop fusion | flops 6553600 | bytes 6597120 | tf_op jit(solution)/shard_map/le | solution.py:102
  155.2 1.2 multiply_reduce_fusion.1
  156.5 26.4 %fusion = (f32[2,640]{1,0:T(2,128)S(1)}, f32[2,640,10240]{2,1,0:T(8,128)}) fusion(pred[640,10240]{1,0:T(8,128)(4,1)} %broadcast_compare_fusion, bf16[10240,2,128]{0,2,1:T(8,128)(2,1)} %bitcast.95, f32[640,3,2,128]{0,3,2,1:T(8,128)} %copy-done.1, f32[128]{0:T(128)S(1)} %get-tuple-element.33, f32[640,2]{0,1:T(2,128)S(1)} %add_rsqrt_fusion.1), kind=kOutput, calls=%fused_computation.5 | convolution fusion | flops 3395255040 | bytes 64891392 | tf_op jit(solution)/shard_map/rhe,khe->hrk/dot_general | solution.py:94
  182.9 18.0 %all-gather.6.cloned.1.call-done = bf16[10240,256]{0,1:T(8,128)(2,1)} async-done(((bf16[640,256]{0,1:T(8,128)(2,1)}), bf16[10240,256]{0,1:T(8,128)(2,1)}) %all-gather.6.cloned.1.call-update) | async-done | bytes 5242896 | tf_op jit(solution)/shard_map/all_gather | solution.py:91
  200.9 22.6 %fusion.15 = bf16[640,2,128]{0,2,1:T(8,128)(2,1)S(1)} fusion(bf16[10240,2,128]{0,2,1:T(8,128)(2,1)} %bitcast.96, f32[2,640,10240]{2,1,0:T(8,128)} %get-tuple-element.36, pred[640,10240]{1,0:T(8,128)(4,1)} %broadcast_compare_fusion, f32[640,2]{0,1:T(2,128)S(1)} %select_bitcast_fusion.2), kind=kOutput, calls=%fused_computation.20 | convolution fusion | flops 3395092480 | bytes 64558080 | tf_op jit(solution)/shard_map/hrk,khe->rhe/dot_general | solution.py:105
  223.5 3.9 %convolution_convert_fusion = bf16[640,4096]{1,0:T(8,128)(2,1)} fusion(bf16[640,256]{0,1:T(8,128)(2,1)S(1)} %bitcast.87, bf16[1,256,4096]{2,1,0:T(8,128)(2,1)S(1)} %copy-done), kind=kOutput, calls=%fused_computation.15 | convolution fusion | flops 1344798720 | bytes 7667712 | tf_op jit(solution)/shard_map/dot_general | solution.py:118
  227.4 2.4 scatter_custom_fusion
  229.9 0.6 compare_select_fusion.1
  230.5 77.9 %reduce-scatter.2.cloned.1.call-done = bf16[640,256]{1,0:T(8,128)(2,1)} async-done(((bf16[640,4096]{1,0:T(8,128)(2,1)}), bf16[640,256]{1,0:T(8,128)(2,1)}) %reduce-scatter.2.cloned.1.call-update) | async-done | bytes 327696 | tf_op jit(solution)/shard_map/reduce_scatter | solution.py:119
  308.5 6.4 %all_to_all.11 = bf16[2,320,256]{2,1,0:T(8,128)(2,1)S(1)} all-to-all(bf16[2,320,256]{2,1,0:T(8,128)(2,1)} %bitcast.88), channel_id=1, replica_groups=mesh['mod'=2,'seq'=8,'tp'=16] {'mod'}, dimensions={0} | all-to-all | bytes 655360 | tf_op jit(solution)/shard_map/all_to_all | solution.py:123
  314.9 2.6 gather_fusion.1
  (91 shorter events, 3.2 us)
Async XLA Ops:
  7.4 216.1 %copy-start = (bf16[1,256,4096]{2,1,0:T(8,128)(2,1)S(1)}, bf16[1,256,4096]{2,1,0:T(8,128)(2,1)}, u32[]{:S(2)}) copy-start(bf16[1,256,4096]{2,1,0:T(8,128)(2,1)} %param.11) | copy-start | bytes 6291460
  7.4 68.8 %all-gather.4.cloned.1.call-start = ((), (), s32[]{:S(2)}) async-start(), calls=%async_computation.3 | async-start | bytes 4456448 | tf_op jit(solution)/shard_map/all_gather | solution.py:66
  8.1 105.4 %sort.37.cloned.1.call-start = ((), (), s32[]{:S(2)}) async-start(), calls=%async_computation.7 | async-start | bytes 196640 | tf_op jit(solution)/shard_map/vmap(jit(argsort))/sort | solution.py:19
  10.2 146.4 %all-gather.8.cloned.1.call-start = ((), (), s32[]{:S(2)}) async-start(), calls=%async_computation.5 | async-start | bytes 5570560 | tf_op jit(solution)/shard_map/all_gather | solution.py:90
  18.8 8.8 %copy-start.3 = (f32[2,4096]{1,0:T(2,128)S(1)}, f32[2,4096]{1,0:T(2,128)}, u32[]{:S(2)}) copy-start(f32[2,4096]{1,0:T(2,128)} %param.8) | copy-start | bytes 98308
  18.8 8.8 %copy-start.4 = (f32[2,2,128]{2,1,0:T(2,128)S(1)}, f32[2,2,128]{2,1,0:T(2,128)}, u32[]{:S(2)}) copy-start(f32[2,2,128]{2,1,0:T(2,128)} %param.10) | copy-start | bytes 6148
  102.6 3.3 %slice-start = ((s8[6291456]{0:T(1024)(128)(4,1)}), s8[4194304]{0:T(1024)(128)(4,1)S(1)}, s32[]{:S(2)}) async-start(s8[6291456]{0:T(1024)(128)(4,1)} %bitcast.82), calls=%async_computation.9 | async-start | bytes 8388608
  103.7 2.1 slice-start.1
  105.8 7.4 %copy-start.2 = (s32[16,512]{1,0:T(8,128)S(1)}, s32[16,512]{1,0:T(8,128)}, u32[]{:S(2)}) copy-start(s32[16,512]{1,0:T(8,128)} %reshape.304) | copy-start | bytes 98308
  110.9 1.3 copy-start.1
  113.2 87.7 %all-gather.6.cloned.1.call-start = ((), (), s32[]{:S(2)}) async-start(), calls=%async_computation.4 | async-start | bytes 5570560 | tf_op jit(solution)/shard_map/all_gather | solution.py:91
  116.9 191.6 %reduce-scatter.2.cloned.1.call-start = ((), (), s32[]{:S(2)}) async-start(), calls=%async_computation.6 | async-start | bytes 5570560 | tf_op jit(solution)/shard_map/reduce_scatter | solution.py:119
Sparse Core Ops, SparseCore 0:
  10.6 65.4 all-gather.3
  113.3 43.1 all-gather.7
  158.3 42.5 all-gather.5
  227.5 80.8 reduce-scatter.1
Sparse Core Ops, SparseCore 1:
  11.0 2.4 sort.39.cloned.1.call-done
  (1 shorter events, 0.0 us)
where the time goes:
time: 326 us; the launch traced here: 325 us
  waiting for transfers between devices  145 us (44%)
  local copies, waits for them, and re-layouts  66.6 us (20%)
  matrix products  57.9 us (18%)
  other arithmetic  21.1 us (6%)
  between operations  17.4 us (5%)
  blocking collectives  15.6 us (5%)
    reduce_scatter x1, waiting for transfers between devices, body(): lax.psum_scatter(head_terms.astype(jnp.bfloat16), 'tp', scatter_dimension...  77.9 us
    all_gather x1, waiting for transfers between devices, body(): gathered = lax.all_gather(tokens, 'tp', axis=1, tiled=True)  48.4 us
    gather x64, local copies, waits for them, and re-layouts  30.5 us
    dot_general x1, matrix products, body(): jnp.einsum('rhe,khe->hrk', query_rows, key_piece.reshape(count, heads_her...  26.4 us
    dot_general x1, matrix products, body(): jnp.einsum('hrk,khe->rhe', rounded, value_piece.reshape(count, heads_here...  22.6 us
    all_gather x1, waiting for transfers between devices, body(): value_piece = lax.all_gather(value_rows, ('mod', 'seq'), axis=0, tiled=True)  18 us
    gather x1, local copies, waits for them, and re-layouts, select_rows(): table[picked]  14.3 us
    unnamed x18, local copies, waits for them, and re-layouts  10.2 us
  transfers between devices with their start and end apart: 4, of which 4 were waited for; matrix products, arithmetic and copies ran while one was open for 27% of the time, Pallas kernels for 0%

commit v1 on v0

v1 whole, which is shorter than its diff:
```python
import math

import jax
import jax.numpy as jnp
from jax import lax
from jax.experimental import pallas as pl
from jax.experimental.pallas import tpu as pltpu
from jax.sharding import PartitionSpec as P

MESH = pl.DeviceIdType.MESH
F32 = jnp.float32
BF16 = jnp.bfloat16
epsilon = 1e-05
SPAN = 64
HD = 128
TOK = 512
W = 256
D = 4096
NH = 1
R = TOK // NH
H = R // 2
Q4 = H // 2
TQ = 256
QSCALE = math.log2(math.e) / math.sqrt(HD)
N_SEM = 256


def kernel(mod_ref, tok_in, gain_ref, w_in, hg_ref, w_out, out_ref,
           tok, wcat, wo, acc, ssq, qbuf, kv, o_acc, l_acc, att, term,
           r1, r2, msg, ubuf, r3, msg4, r4, fin, fin_in,
           send_sem, recv_sem, loc_sem):
    m = lax.axis_index("mod")
    z = lax.axis_index("seq")
    tp = lax.axis_index("tp")
    sib = 1 - m
    sa = 4 - 3 * m
    sb = 1 + 3 * m
    a = lax.rem(lax.div(tp, sa), 4)
    b = lax.rem(lax.div(tp, sb), 4)

    def slot(i, k):
        return lax.rem(a + i, 4) * sa + lax.rem(b + k, 4) * sb

    a_next, a_prev = {"tp": slot(1, 0)}, {"tp": slot(3, 0)}
    b_next, b_prev = {"tp": slot(0, 1)}, {"tp": slot(0, 3)}
    z_next, z_prev = {"seq": lax.rem(z + 1, 8)}, {"seq": lax.rem(z + 7, 8)}
    other = {"mod": sib}

    barrier = pltpu.get_barrier_semaphore()
    for dev in (a_next, a_prev, b_next, b_prev, z_next, z_prev, other):
        pl.semaphore_signal(barrier, inc=1, device_id=dev, device_id_type=MESH)
    pl.semaphore_wait(barrier, 7)

    sent = []
    count = [0]

    def send(src, dst, dev):
        i = count[0]
        count[0] += 1
        copy = pltpu.make_async_remote_copy(
            src_ref=src, dst_ref=dst, send_sem=send_sem.at[i], recv_sem=recv_sem.at[i],
            device_id=dev, device_id_type=MESH)
        copy.start()
        sent.append(copy)
        return copy

    def span_mod(c, block):
        s, h = divmod(c, NH)
        return mod_ref[(s * 8 + z) * TOK + h * R + block * SPAN]

    def pick(flag, one, zero):
        return jnp.where(jnp.full(one.shape, flag, jnp.int32) == 1, one, zero)

    tme = slot(0, 0)
    swap = []
    own_copies = []
    for h in range(NH):
        src = tok_in.at[pl.ds(h * R, R), :]
        dst = tok.at[m * NH + h, tme]
        swap.append(send(src, dst, other))
        cp = pltpu.make_async_copy(src, dst, loc_sem.at[h])
        cp.start()
        own_copies.append(cp)

    w_local = []
    w_remote = []
    for p in range(3):
        cp = pltpu.make_async_copy(
            w_in.at[p, :, pl.ds(pl.multiple_of(m * HD, HD), HD)],
            wcat.at[:, pl.ds(p * HD, HD)], loc_sem.at[NH + p])
        cp.start()
        w_local.append(cp)
        w_remote.append(send(
            w_in.at[p, :, pl.ds(pl.multiple_of(sib * HD, HD), HD)],
            wcat.at[:, pl.ds(384 + p * HD, HD)], other))

    def gather(c):
        rows = pl.ds(pl.multiple_of(m * H, H), H)
        low = pl.ds(pl.multiple_of(m * H, Q4), Q4)
        high = pl.ds(pl.multiple_of(m * H + Q4, Q4), Q4)

        def put(t, part, dev):
            ref = tok.at[c, t, part]
            return send(ref, ref, dev)

        acc[...] = jnp.zeros_like(acc)
        ssq[...] = jnp.zeros_like(ssq)
        own = slot(0, 0)
        ar = put(own, rows, a_next)
        al = put(own, rows, a_prev)
        bn, bp = {}, {}
        bn[0] = put(own, rows, b_next)
        bp[0] = put(own, rows, b_prev)
        yield
        d2d = {}
        ar.wait_recv()
        f1 = put(slot(3, 0), low, a_next)
        bn[3] = put(slot(3, 0), rows, b_next)
        bp[3] = put(slot(3, 0), rows, b_prev)
        d2d[3, 0] = put(slot(3, 0), rows, other)
        al.wait_recv()
        f2 = put(slot(1, 0), high, a_prev)
        bn[1] = put(slot(1, 0), rows, b_next)
        bp[1] = put(slot(1, 0), rows, b_prev)
        d2d[1, 0] = put(slot(1, 0), rows, other)
        yield
        f1.wait_recv()
        f2.wait_recv()
        bn[2] = put(slot(2, 0), rows, b_next)
        bp[2] = put(slot(2, 0), rows, b_prev)
        d2d[2, 0] = put(slot(2, 0), rows, other)
        yield
        g1, g2 = {}, {}
        for i in (0, 3, 1, 2):
            bn[i].wait_recv()
            g1[i] = put(slot(i, 3), low, b_next)
            d2d[i, 3] = put(slot(i, 3), rows, other)
            bp[i].wait_recv()
            g2[i] = put(slot(i, 1), high, b_prev)
            d2d[i, 1] = put(slot(i, 1), rows, other)
        yield
        for i in (1, 2, 3):
            d2d[i, 0].wait_recv()
        pairs(c, 3, lambda n: (n + 1, 0))
        for i in range(4):
            d2d[i, 1].wait_recv()
            d2d[i, 3].wait_recv()
        pairs(c, 8, lambda n: (lax.rem(n, 4), 1 + 2 * lax.div(n, 4)))
        for i in (0, 3, 1, 2):
            g1[i].wait_recv()
            g2[i].wait_recv()
            d2d[i, 2] = put(slot(i, 2), rows, other)
        yield
        for i in range(4):
            d2d[i, 2].wait_recv()
        pairs(c, 4, lambda n: (n, 2))
        yield

    def unit(c, t, j):
        start = pl.multiple_of(j * H, H)
        rows = pl.ds(start, H)
        x = tok[c, t, rows, :]
        first = pl.multiple_of(t * W, W)
        g = gain_ref[:, pl.ds(first, W)]
        scaled, squares = [], []
        for k in range(H // SPAN):
            flag = span_mod(c, j * (H // SPAN) + k)
            xb = x[k * SPAN:(k + 1) * SPAN].astype(F32)
            sq = xb * xb
            squares.append(sq[:, :128] + sq[:, 128:])
            scaled.append((xb * pick(flag, g[1:2], g[0:1])).astype(BF16))
        ssq[rows, :] += jnp.concatenate(squares, axis=0)
        acc[rows, :] += jnp.dot(jnp.concatenate(scaled, axis=0), wcat[pl.ds(first, W), :],
                                preferred_element_type=F32)

    def pairs(c, n, where):
        def step(q, carry):
            i, k = where(q)
            unit(c, slot(i, k), m)
            unit(c, slot(k, i), sib)
            return carry
        lax.fori_loop(0, n, step, 0)

    def own_unit(c):
        def step(j, carry):
            unit(c, slot(0, 0), j)
            return carry
        lax.fori_loop(0, 2, step, 0)

    def finish_qkv(c):
        def step(k, carry):
            r0 = pl.multiple_of(k * SPAN, SPAN)
            flag = span_mod(c, k)
            mine = (jnp.full((SPAN, 3 * HD), flag, jnp.int32) == m)
            block = acc[pl.ds(r0, SPAN), :]
            block = jnp.where(mine, block[:, :3 * HD], block[:, 3 * HD:])
            mean = jnp.sum(ssq[pl.ds(r0, SPAN), :], axis=1, keepdims=True) * (1.0 / D)
            block = block * lax.rsqrt(mean + epsilon)
            qp, kp, vp = block[:, :HD], block[:, HD:2 * HD], block[:, 2 * HD:]
            qg = pick(flag, hg_ref[1, 0:1], hg_ref[0, 0:1])
            kg = pick(flag, hg_ref[1, 1:2], hg_ref[0, 1:2])
            qm = jnp.mean(qp * qp, axis=1, keepdims=True)
            km = jnp.mean(kp * kp, axis=1, keepdims=True)
            qbuf[pl.ds(c * R + r0, SPAN), :] = (qp * lax.rsqrt(qm + epsilon) * (qg * QSCALE)).astype(BF16)
            kv[c, z, pl.ds(r0, SPAN), 0:HD] = (kp * lax.rsqrt(km + epsilon) * kg).astype(BF16)
            kv[c, z, pl.ds(r0, SPAN), HD:2 * HD] = vp.astype(BF16)
            return carry
        lax.fori_loop(0, R // SPAN, step, 0)

    low_half = pl.ds(0, R // 2)
    high_half = pl.ds(R // 2, R // 2)

    def zring(c):
        def put(src_z, part, dev):
            ref = kv.at[c, lax.rem(src_z, 8), part]
            return send(ref, ref, dev)
        full = pl.ds(0, R)
        right = put(z, full, z_next)
        left = put(z, full, z_prev)
        yield
        for d in (1, 2, 3):
            right.wait_recv()
            right = put(z + 8 - d, full if d < 3 else low_half, z_next)
            left.wait_recv()
            left = put(z + d, full if d < 3 else high_half, z_prev)
            yield
        right.wait_recv()
        left.wait_recv()
        yield

    def tile(c, src, r0, diagonal):
        rows = pl.ds(r0, TQ)
        s = lax.dot_general(qbuf[rows, :], kv[c, src, :, 0:HD], (((1,), (1,)), ((), ())),
                            preferred_element_type=F32)
        p = jnp.exp2(s)
        if diagonal:
            at = lax.broadcasted_iota(jnp.int32, p.shape, 0) + (r0 - c * R)
            p = jnp.where(lax.broadcasted_iota(jnp.int32, p.shape, 1) <= at, p, 0.0)
        total = p[:, 0:128]
        for k in range(1, R // 128):
            total = total + p[:, k * 128:(k + 1) * 128]
        l_acc[rows, :] += total
        o_acc[rows, :] += jnp.dot(p.astype(BF16), kv[c, src, :, HD:2 * HD], preferred_element_type=F32)

    def attend(c, src, lo, hi, diagonal=False):
        def step(n, carry):
            tile(c, src, pl.multiple_of(n * TQ, TQ), diagonal)
            return carry
        lax.fori_loop(lo, hi, step, 0)

    half = TOK // TQ

    def attend_own(c):
        first = c * R // TQ
        attend(c, z, first, first + R // TQ, True)
        if first + R // TQ < 2 * half:
            attend(c, z, first + R // TQ, 2 * half)

    def attend_from(c, src):
        if c < NH:
            attend(c, src, jnp.where(src < z, 0, half), 2 * half)
        else:
            attend(c, src, jnp.where(src < z, half, 2 * half), 2 * half)

    def attend_step(c, d):
        attend_from(c, lax.rem(z + 8 - d, 8))
        if d < 4:
            attend_from(c, lax.rem(z + d, 8))

    def reduce(c):
        rows = pl.ds(c * R, R)
        total = jnp.sum(l_acc[rows, :], axis=1, keepdims=True)
        att[c, m] = (o_acc[rows, :] / total).astype(BF16)
        ref = att.at[c, m]
        swapped = send(ref, ref, other)
        yield
        swapped.wait_recv()

        def product(g):
            def step(k, carry):
                r0 = pl.multiple_of(k * 128, 128)
                left, right = [], []
                for n in range(2):
                    flag = span_mod(c, k * 2 + n)
                    mine = (jnp.full((SPAN, HD), flag, jnp.int32) == m)
                    parts = [att[c, h, pl.ds(r0 + n * SPAN, SPAN), :] for h in range(2)]
                    zero = jnp.zeros((SPAN, HD), BF16)
                    left.append(jnp.concatenate([jnp.where(mine, q, zero) for q in parts], axis=1))
                    right.append(jnp.concatenate([jnp.where(mine, zero, q) for q in parts], axis=1))
                lhs = jnp.concatenate(
                    [jnp.concatenate(left, axis=0), jnp.concatenate(right, axis=0)], axis=1)
                res = jnp.dot(lhs, wo[lax.rem(a + g, 4)], preferred_element_type=F32).astype(BF16)
                for k4 in range(4):
                    term[c, g, k4, pl.ds(r0, 128), :] = res[:, k4 * 128:(k4 + 1) * 128]
                return carry
            lax.fori_loop(0, R // 128, step, 0)

        product(2)
        s1 = send(term.at[c, 2, :, low_half], r1.at[c, 0], a_next)
        s2 = send(term.at[c, 2, :, high_half], r1.at[c, 1], a_prev)

        def rest(n, carry):
            product(jnp.where(n == 2, 0, 2 * n + 1))
            return carry
        lax.fori_loop(0, 3, rest, 0)
        yield

        def add(x, y):
            return (x.astype(F32) + y.astype(F32)).astype(BF16)

        s1.wait_recv()
        msg[c, 0, :, low_half] = add(term[c, 1, :, low_half], r1[c, 0])
        msg[c, 0, :, high_half] = term[c, 1, :, high_half]
        s3 = send(msg.at[c, 0], r2.at[c, 0], a_next)
        s2.wait_recv()
        msg[c, 1, :, high_half] = add(term[c, 3, :, high_half], r1[c, 1])
        msg[c, 1, :, low_half] = term[c, 3, :, low_half]
        s4 = send(msg.at[c, 1], r2.at[c, 1], a_prev)
        yield
        s3.wait_recv()
        s4.wait_recv()

        def total4(k, carry):
            ubuf[c, k] = (term[c, 0, k].astype(F32) + r2[c, 0, k].astype(F32)
                          + r2[c, 1, k].astype(F32)).astype(BF16)
            return carry

        total4(lax.rem(b + 2, 4), 0)
        s5 = send(ubuf.at[c, lax.rem(b + 2, 4), low_half], r3.at[c, 0], b_next)
        s6 = send(ubuf.at[c, lax.rem(b + 2, 4), high_half], r3.at[c, 1], b_prev)
        total4(lax.rem(b + 1, 4), 0)
        total4(lax.rem(b + 3, 4), 0)
        total4(b, 0)
        yield
        s5.wait_recv()
        up, down = lax.rem(b + 1, 4), lax.rem(b + 3, 4)
        msg4[c, 0, low_half] = add(ubuf[c, up, low_half], r3[c, 0])
        msg4[c, 0, high_half] = ubuf[c, up, high_half]
        s7 = send(msg4.at[c, 0], r4.at[c, 0], b_next)
        s6.wait_recv()
        msg4[c, 1, high_half] = add(ubuf[c, down, high_half], r3[c, 1])
        msg4[c, 1, low_half] = ubuf[c, down, low_half]
        s8 = send(msg4.at[c, 1], r4.at[c, 1], b_prev)
        yield
        s7.wait_recv()
        s8.wait_recv()
        fin[c] = (ubuf[c, b].astype(F32) + r4[c, 0].astype(F32) + r4[c, 1].astype(F32)).astype(BF16)
        yield

    def go(stream, n=1):
        for _ in range(n):
            next(stream)

    for cp in own_copies:
        cp.wait()
    for cp in swap:
        cp.wait_recv()
    gathers = [gather(c) for c in range(2 * NH)]
    rings = [zring(c) for c in range(2 * NH)]
    sums = [reduce(c) for c in range(2 * NH)]

    go(gathers[0], 1)
    wo_local = []
    for i in range(4):
        for k in range(4):
            t = i * sa + k * sb
            cp = pltpu.make_async_copy(
                w_out.at[:, pl.ds(pl.multiple_of(t * W + m * HD, HD), HD)],
                wo.at[i, pl.ds(0, 256), pl.ds(k * HD, HD)], loc_sem.at[NH + 3 + i * 4 + k])
            cp.start()
            wo_local.append(cp)
    wo_remote = []
    o_acc[...] = jnp.zeros_like(o_acc)
    l_acc[...] = jnp.zeros_like(l_acc)
    go(gathers[0], 2)
    for cp in w_local:
        cp.wait()
    for cp in w_remote:
        cp.wait_recv()
    own_unit(0)
    go(gathers[0], 3)
    for i in range(4):
        for k in range(4):
            t = i * sb + k * sa
            wo_remote.append(send(
                w_out.at[:, pl.ds(pl.multiple_of(t * W + sib * HD, HD), HD)],
                wo.at[i, pl.ds(256, 256), pl.ds(k * HD, HD)], other))
    finish_qkv(0)
    go(rings[0])
    go(gathers[1])
    own_unit(1)
    go(gathers[1], 2)
    go(rings[0])
    go(gathers[1], 1)
    go(gathers[1], 2)
    finish_qkv(1)
    go(rings[1])
    go(rings[0])
    attend_own(0)
    attend_step(0, 1)
    go(rings[0])
    attend_step(0, 2)
    attend_own(1)
    go(rings[0])
    go(rings[1])
    attend_step(0, 3)
    attend_step(0, 4)
    for cp in wo_local:
        cp.wait()
    for cp in wo_remote:
        cp.wait_recv()
    go(sums[0])
    attend_step(1, 1)
    go(sums[0])
    go(rings[1])
    go(sums[0])
    attend_step(1, 2)
    go(rings[1])
    go(sums[0])
    attend_step(1, 3)
    go(sums[0])
    go(rings[1])
    attend_step(1, 4)
    go(sums[1], 1)
    go(sums[0], 1)
    go(sums[1], 5)

    back = []
    for h in range(NH):
        back.append(send(fin.at[sib * NH + h], fin_in.at[h], other))
    for h in range(NH):
        back[h].wait_recv()
        own = fin[m * NH + h]
        got = fin_in[h]
        lower = jnp.full(own.shape, m, jnp.int32) == 0
        out_ref[h * R:(h + 1) * R, 0:HD] = jnp.where(lower, own, got)
        out_ref[h * R:(h + 1) * R, HD:2 * HD] = jnp.where(lower, got, own)
    for cp in sent:
        cp.wait_send()


def body(tokens, modality, norm_gain, input_weight, head_gain, output_weight):
    chunks = 2 * NH
    vmem = pl.BlockSpec(memory_space=pltpu.VMEM)
    anywhere = pl.BlockSpec(memory_space=pl.ANY)
    w3 = jnp.transpose(input_weight[0], (1, 0, 2))
    return pl.pallas_call(
        kernel,
        out_shape=jax.ShapeDtypeStruct((TOK, W), BF16),
        in_specs=[pl.BlockSpec(memory_space=pltpu.SMEM), vmem, vmem, anywhere, vmem, anywhere],
        out_specs=vmem,
        scratch_shapes=[
            pltpu.VMEM((chunks, 16, R, W), BF16),
            pltpu.VMEM((D, 6 * HD), BF16),
            pltpu.VMEM((4, 512, 512), BF16),
            pltpu.VMEM((R, 6 * HD), F32),
            pltpu.VMEM((R, 128), F32),
            pltpu.VMEM((2 * TOK, HD), BF16),
            pltpu.VMEM((chunks, 8, R, 2 * HD), BF16),
            pltpu.VMEM((2 * TOK, HD), F32),
            pltpu.VMEM((2 * TOK, 128), F32),
            pltpu.VMEM((chunks, 2, R, HD), BF16),
            pltpu.VMEM((chunks, 4, 4, R, 128), BF16),
            pltpu.VMEM((chunks, 2, 4, R // 2, 128), BF16),
            pltpu.VMEM((chunks, 2, 4, R, 128), BF16),
            pltpu.VMEM((chunks, 2, 4, R, 128), BF16),
            pltpu.VMEM((chunks, 4, R, 128), BF16),
            pltpu.VMEM((chunks, 2, R // 2, 128), BF16),
            pltpu.VMEM((chunks, 2, R, 128), BF16),
            pltpu.VMEM((chunks, 2, R, 128), BF16),
            pltpu.VMEM((chunks, R, 128), BF16),
            pltpu.VMEM((NH, R, 128), BF16),
            pltpu.SemaphoreType.DMA((N_SEM,)),
            pltpu.SemaphoreType.DMA((N_SEM,)),
            pltpu.SemaphoreType.DMA((NH + 3 + 16,)),
        ],
        compiler_params=pltpu.CompilerParams(
            collective_id=0, has_side_effects=True, vmem_limit_bytes=56 * 1024 * 1024),
    )(modality, tokens, norm_gain, w3, head_gain, output_weight[0])


def solution(mesh):
    in_specs = (
        P(("mod", "seq"), "tp"),
        P(),
        P(),
        P("mod", None, None, "tp"),
        P(),
        P("mod", "tp", None),
    )
    out_specs = P(("mod", "seq"), "tp")
    return jax.shard_map(body, mesh=mesh, in_specs=in_specs, out_specs=out_specs, check_vma=False)
```

time: 326 us -> 136 us (0.42)
  waiting for transfers between devices: 145 us -> 0 us
  Pallas kernels: 0 us -> 133 us
  local copies, waits for them, and re-layouts: 66.6 us -> 1.67 us
  matrix products: 57.9 us -> 0 us
  other arithmetic: 21.1 us -> 0 us
  between operations: 17.4 us -> 0.01 us
  blocking collectives: 15.6 us -> 0 us
    pallas_call x0 -> x1, Pallas kernels: none -> 133 us  [body(): pl.pallas_call(kernel, out_shape=jax.ShapeDtypeStruct((TOK, W), BF16), in...]
    reduce_scatter x1 -> x0, waiting for transfers between devices: 77.9 us -> none  [body(): lax.psum_scatter(head_terms.astype(jnp.bfloat16), 'tp', scatter_dimension...]
    all_gather x3 -> x0, waiting for transfers between devices: 66.5 us -> none  [the longest x1 48.4 us: body(): gathered = lax.all_gather(tokens, 'tp', axis=1, tiled=True)]
    dot_general x4 -> x0, matrix products: 57.9 us -> none  [the longest x1 26.4 us: body(): jnp.einsum('rhe,khe->hrk', query_rows, key_piece.reshape(count, heads_her...]
    gather x66 -> x0, local copies, waits for them, and re-layouts: 47.4 us -> none
    all_to_all x2 -> x0, blocking collectives: 15.6 us -> none  [the longest x1 9.17 us: body(): lax.all_to_all(select_rows(gathered, picked, live), 'mod', split_axis=0,...]
    unnamed x18 -> x1, local copies, waits for them, and re-layouts: 10.2 us -> 1.67 us
    le x1 -> x0, other arithmetic: 6.85 us -> none  [body(): key_order[None, None, :] <= own_query[None, :, None]]
  transfers between devices with their start and end apart: 4 -> 0, of which waited for: 4 -> 0; matrix products, arithmetic and copies ran while one was open for 27% -> 0% of each run, Pallas kernels for 0% -> 0%
where the time goes in v1:
time: 136 us; the launch traced here: 135 us
  Pallas kernels  133 us (98%)
  local copies, waits for them, and re-layouts  1.67 us (1%)
    pallas_call x1, Pallas kernels, body(): pl.pallas_call(kernel, out_shape=jax.ShapeDtypeStruct((TOK, W), BF16), in...  133 us

profile of v1, /device:TPU:1, one launch (start us, length us, event | category | flops | bytes accessed | tf_op | source)
XLA Modules:
  0.0 135.1 jit_solution(15273457717357551850)
XLA Ops:
  0.0 133.5 %shard_map.64 = bf16[512,256]{1,0:T(8,128)(2,1)} custom-call(s32[8192]{0:T(1024)} %mod_ref.1, bf16[512,256]{1,0:T(8,128)(2,1)} %tok_in.1, f32[2,4096]{1,0:T(2,128)} %gain_ref.1, bf16[3,4096,256]{2,1,0:T(8,128)(2,1)} %bitcast.4, f32[2,2,128]{2,1,0:T(2,128)} %hg_ref.1, bf16[256,4096]{1,0:T(8,128)(2,1)} %bitcast.5), custom_call_target="tpu_custom_call" | custom-call | tf_op jit(solution)/shard_map/pallas_call | solution.py:447
  133.5 1.7 %copy.8 = bf16[512,256]{1,0:T(8,128)(2,1)} copy(bf16[512,256]{1,0:T(8,128)(2,1)} %shard_map.64) | data formatting | bytes 524288

commit v2 on v1

v2 whole, which is shorter than its diff:
```python
import math

import jax
import jax.numpy as jnp
from jax import lax
from jax.experimental import pallas as pl
from jax.experimental.pallas import tpu as pltpu
from jax.sharding import PartitionSpec as P

MESH = pl.DeviceIdType.MESH
F32 = jnp.float32
BF16 = jnp.bfloat16
epsilon = 1e-05
SPAN = 64
HD = 128
TOK = 512
W = 256
D = 4096
NH = 2
R = TOK // NH
H = R // 2
Q4 = H // 2
TQ = 256
ORDER = (
    "G0", "G0", "G0", "Q0", "Q1", "Q2", "Q3", "G0", "G0", "G0", "G1", "G0", "Q0", "G0", "Q0", "G0",
    "G0", "G1", "G1", "G0", "G0", "Q0", "G1", "G1", "G1", "G2", "G1", "Q0", "Q0", "Z0", "Q1", "Q1",
    "G1", "G1", "G1", "G2", "G2", "G1", "G1", "Z0", "Z0", "Q1", "G2", "G2", "G2", "G2", "G3", "Q1",
    "Q1", "Z1", "Q2", "Q2", "Z0", "Z0", "G2", "G2", "G2", "G2", "ALL0", "G3", "G3", "G2", "Z1", "Z1",
    "ALL1", "Q2", "G3", "G3", "G3", "G3", "Q2", "Z0", "Z0", "Q2", "Z2", "Q3", "Q3", "Z1", "Z1", "G3",
    "G3", "G3", "G3", "ALL2", "G3", "Q3", "Z2", "Z2", "Q3", "Q3", "Z3", "AUU0", "Z1", "Z1", "ALL3", "ALU0",
    "ALU1", "Z2", "Z2", "ALU2", "ALU3", "Z3", "Z3", "AUU1", "ALL4", "R0", "R1", "ALU4", "R0", "R0", "Z2", "Z2",
    "R1", "R1", "Z3", "Z3", "AUU2", "R0", "R0", "R1", "R1", "Z3", "Z3", "AUU3", "R0", "R0", "AUU4", "R2",
    "R3", "R0", "R1", "R0", "R1", "R2", "R2", "R3", "R3", "R0", "R1", "R1", "R2", "R2", "R3", "R3",
    "R1", "R2", "R2", "R3", "R2", "R3", "R2", "R3", "R3", "R2", "R3",
)
QSCALE = math.log2(math.e) / math.sqrt(HD)
N_SEM = 256


def kernel(mod_ref, tok_in, gain_ref, w_in, hg_ref, w_out, out_ref,
           tok, wcat, wo, acc, ssq, qbuf, kv, o_acc, l_acc, att, term,
           abuf, r1, r2, msg, ubuf, r3, msg4, r4, fin, fin_in,
           send_sem, recv_sem, loc_sem):
    m = lax.axis_index("mod")
    z = lax.axis_index("seq")
    tp = lax.axis_index("tp")
    sib = 1 - m
    sa = 4 - 3 * m
    sb = 1 + 3 * m
    a = lax.rem(lax.div(tp, sa), 4)
    b = lax.rem(lax.div(tp, sb), 4)

    def slot(i, k):
        return lax.rem(a + i, 4) * sa + lax.rem(b + k, 4) * sb

    a_next, a_prev = {"tp": slot(1, 0)}, {"tp": slot(3, 0)}
    b_next, b_prev = {"tp": slot(0, 1)}, {"tp": slot(0, 3)}
    z_next, z_prev = {"seq": lax.rem(z + 1, 8)}, {"seq": lax.rem(z + 7, 8)}
    other = {"mod": sib}

    barrier = pltpu.get_barrier_semaphore()
    for dev in (a_next, a_prev, b_next, b_prev, z_next, z_prev, other):
        pl.semaphore_signal(barrier, inc=1, device_id=dev, device_id_type=MESH)
    pl.semaphore_wait(barrier, 7)

    sent = []
    count = [0]

    def send(src, dst, dev):
        i = count[0]
        count[0] += 1
        copy = pltpu.make_async_remote_copy(
            src_ref=src, dst_ref=dst, send_sem=send_sem.at[i], recv_sem=recv_sem.at[i],
            device_id=dev, device_id_type=MESH)
        copy.start()
        sent.append(copy)
        return copy

    landed = set()

    def arrive(*copies):
        for copy in copies:
            if id(copy) not in landed:
                landed.add(id(copy))
                copy.wait_recv()

    def span_mod(c, block):
        s, h = divmod(c, NH)
        return mod_ref[(s * 8 + z) * TOK + h * R + block * SPAN]

    def pick(flag, one, zero):
        return jnp.where(jnp.full(one.shape, flag, jnp.int32) == 1, one, zero)

    tme = slot(0, 0)
    swap = []
    own_copies = []
    for h in range(NH):
        src = tok_in.at[pl.ds(h * R, R), :]
        dst = tok.at[m * NH + h, tme]
        swap.append(send(src, dst, other))
        cp = pltpu.make_async_copy(src, dst, loc_sem.at[h])
        cp.start()
        own_copies.append(cp)

    w_local = []
    w_remote = []
    for p in range(3):
        cp = pltpu.make_async_copy(
            w_in.at[p, :, pl.ds(pl.multiple_of(m * HD, HD), HD)],
            wcat.at[:, pl.ds(p * HD, HD)], loc_sem.at[NH + p])
        cp.start()
        w_local.append(cp)
        w_remote.append(send(
            w_in.at[p, :, pl.ds(pl.multiple_of(sib * HD, HD), HD)],
            wcat.at[:, pl.ds(384 + p * HD, HD)], other))

    hops = {}

    def gather(c):
        rows = pl.ds(pl.multiple_of(m * H, H), H)
        low = pl.ds(pl.multiple_of(m * H, Q4), Q4)
        high = pl.ds(pl.multiple_of(m * H + Q4, Q4), Q4)

        def put(t, part, dev):
            ref = tok.at[c, t, part]
            return send(ref, ref, dev)

        own = slot(0, 0)
        ar = put(own, rows, a_next)
        al = put(own, rows, a_prev)
        bn, bp = {}, {}
        d2d = hops[c] = {}
        bn[0] = put(own, rows, b_next)
        bp[0] = put(own, rows, b_prev)
        yield
        arrive(ar)
        f1 = put(slot(3, 0), low, a_next)
        bn[3] = put(slot(3, 0), rows, b_next)
        bp[3] = put(slot(3, 0), rows, b_prev)
        d2d[3, 0] = put(slot(3, 0), rows, other)
        yield
        arrive(al)
        f2 = put(slot(1, 0), high, a_prev)
        bn[1] = put(slot(1, 0), rows, b_next)
        bp[1] = put(slot(1, 0), rows, b_prev)
        d2d[1, 0] = put(slot(1, 0), rows, other)
        yield
        arrive(f1, f2)
        bn[2] = put(slot(2, 0), rows, b_next)
        bp[2] = put(slot(2, 0), rows, b_prev)
        d2d[2, 0] = put(slot(2, 0), rows, other)
        yield
        g1, g2 = {}, {}
        for i in (0, 3, 1, 2):
            arrive(bn[i])
            g1[i] = put(slot(i, 3), low, b_next)
            d2d[i, 3] = put(slot(i, 3), rows, other)
            arrive(bp[i])
            g2[i] = put(slot(i, 1), high, b_prev)
            d2d[i, 1] = put(slot(i, 1), rows, other)
            yield
        for i in (0, 3, 1, 2):
            arrive(g1[i], g2[i])
            d2d[i, 2] = put(slot(i, 2), rows, other)
            yield

    def unit(c, t):
        x = tok[c, t]
        first = pl.multiple_of(t * W, W)
        g = gain_ref[:, pl.ds(first, W)]
        scaled, squares = [], []
        for k in range(R // SPAN):
            flag = span_mod(c, k)
            xb = x[k * SPAN:(k + 1) * SPAN].astype(F32)
            sq = xb * xb
            squares.append(sq[:, :128] + sq[:, 128:])
            scaled.append((xb * pick(flag, g[1:2], g[0:1])).astype(BF16))
        return (jnp.concatenate(squares, axis=0),
                jnp.dot(jnp.concatenate(scaled, axis=0), wcat[pl.ds(first, W), :],
                        preferred_element_type=F32))

    def units(c, n, where):
        def step(q, carry):
            i, k = where(q)
            squares, part = unit(c, slot(i, k))
            ssq[c] += squares
            acc[c] += part
            return carry
        lax.fori_loop(0, n, step, 0)

    def project(c):
        ssq[c], acc[c] = unit(c, slot(0, 0))
        yield
        d2d = hops[c]
        near = [(i, k) for i in (0, 1, 3) for k in (0, 1, 3) if (i, k) != (0, 0)]

        def grid9(q):
            i, k = lax.div(q, 3), lax.rem(q, 3)
            return i + lax.div(i, 2), k + lax.div(k, 2)

        arrive(*[d2d[p] for p in near])
        units(c, 4, lambda q: grid9(q + 1))
        yield
        units(c, 4, lambda q: grid9(q + 5))
        yield
        arrive(*[d2d[i, k] for i in range(4) for k in range(4) if 2 in (i, k)])
        units(c, 4, lambda q: (2, q))
        yield
        units(c, 3, lambda q: (q + lax.div(q, 2), 2))
        yield
        finish_qkv(c)
        yield

    def finish_qkv(c):
        def step(k, carry):
            r0 = pl.multiple_of(k * SPAN, SPAN)
            flag = span_mod(c, k)
            mine = (jnp.full((SPAN, 3 * HD), flag, jnp.int32) == m)
            block = acc[c, pl.ds(r0, SPAN), :]
            block = jnp.where(mine, block[:, :3 * HD], block[:, 3 * HD:])
            mean = jnp.sum(ssq[c, pl.ds(r0, SPAN), :], axis=1, keepdims=True) * (1.0 / D)
            block = block * lax.rsqrt(mean + epsilon)
            qp, kp, vp = block[:, :HD], block[:, HD:2 * HD], block[:, 2 * HD:]
            qg = pick(flag, hg_ref[1, 0:1], hg_ref[0, 0:1])
            kg = pick(flag, hg_ref[1, 1:2], hg_ref[0, 1:2])
            qm = jnp.mean(qp * qp, axis=1, keepdims=True)
            km = jnp.mean(kp * kp, axis=1, keepdims=True)
            qbuf[pl.ds(c * R + r0, SPAN), :] = (qp * lax.rsqrt(qm + epsilon) * (qg * QSCALE)).astype(BF16)
            kv[c // NH, z, pl.ds(c % NH * R + r0, SPAN), 0:HD] = (kp * lax.rsqrt(km + epsilon) * kg).astype(BF16)
            kv[c // NH, z, pl.ds(c % NH * R + r0, SPAN), HD:2 * HD] = vp.astype(BF16)
            return carry
        lax.fori_loop(0, R // SPAN, step, 0)

    ring = {}

    def zring(c):
        def put(src_z, first, count, dev):
            ref = kv.at[c // NH, lax.rem(src_z, 8), pl.ds(c % NH * R + first, count)]
            return send(ref, ref, dev)

        ring[c, "r", 1] = put(z, 0, R, z_next)
        ring[c, "l", 1] = put(z, 0, R, z_prev)
        yield
        for d in (1, 2, 3):
            count = R if d < 3 else R // 2
            arrive(ring[c, "r", d])
            ring[c, "r", d + 1] = put(z + 8 - d, 0, count, z_next)
            yield
            arrive(ring[c, "l", d])
            ring[c, "l", d + 1] = put(z + d, R - count, count, z_prev)
            yield

    def tile(shard, src, r0, diagonal):
        rows = pl.ds(r0, TQ)
        s = lax.dot_general(qbuf[rows, :], kv[shard, src, :, 0:HD], (((1,), (1,)), ((), ())),
                            preferred_element_type=F32)
        p = jnp.exp2(s)
        if diagonal:
            at = lax.broadcasted_iota(jnp.int32, p.shape, 0) + (r0 - shard * TOK)
            p = jnp.where(lax.broadcasted_iota(jnp.int32, p.shape, 1) <= at, p, 0.0)
        total = p[:, 0:128]
        for k in range(1, TOK // 128):
            total = total + p[:, k * 128:(k + 1) * 128]
        l_acc[rows, :] += total
        o_acc[rows, :] += jnp.dot(p.astype(BF16), kv[shard, src, :, HD:2 * HD], preferred_element_type=F32)

    half = TOK // TQ

    def attend(shard, target, d):
        first = target * half
        if d == 0:
            def own(n, carry):
                tile(shard, z, pl.multiple_of(n * TQ, TQ), shard == target)
                return carry
            lax.fori_loop(first, first + half, own, 0)
            return
        for h in range(NH):
            arrive(ring[shard * NH + h, "r", d], ring[shard * NH + h, "l", d])

        def side(q, carry):
            src = lax.rem(z + 8 - d + q * 2 * d, 8)

            def step(n, inner):
                tile(shard, src, pl.multiple_of(n * TQ, TQ), False)
                return inner
            seen = first + half if shard < target else jnp.where(src < z, first + half, first)
            lax.fori_loop(first, seen, step, 0)
            return carry
        lax.fori_loop(0, 2 if d < 4 else 1, side, 0)

    low_half = pl.ds(0, R // 2)
    high_half = pl.ds(R // 2, R // 2)

    def reduce(c):
        rows = pl.ds(c * R, R)
        total = jnp.sum(l_acc[rows, :], axis=1, keepdims=True)
        att[c, m] = (o_acc[rows, :] / total).astype(BF16)
        ref = att.at[c, m]
        swapped = send(ref, ref, other)
        yield
        arrive(swapped)

        zero = jnp.zeros((SPAN, HD), BF16)
        for n in range(R // SPAN):
            mine = (jnp.full((SPAN, HD), span_mod(c, n), jnp.int32) == m)
            for h in range(2):
                part = att[c, h, n * SPAN:(n + 1) * SPAN, :]
                abuf[c, n * SPAN:(n + 1) * SPAN, h * HD:(h + 1) * HD] = jnp.where(mine, part, zero)
                abuf[c, n * SPAN:(n + 1) * SPAN, 256 + h * HD:256 + (h + 1) * HD] = jnp.where(mine, zero, part)

        def product(g):
            res = jnp.dot(abuf[c], wo[lax.rem(a + g, 4)], preferred_element_type=F32).astype(BF16)
            for k4 in range(4):
                term[c, g, k4] = res[:, k4 * 128:(k4 + 1) * 128]

        product(2)
        s1 = send(term.at[c, 2, :, low_half], r1.at[c, 0], a_next)
        s2 = send(term.at[c, 2, :, high_half], r1.at[c, 1], a_prev)
        yield

        def rest(n, carry):
            product(jnp.where(n == 2, 0, 2 * n + 1))
            return carry
        lax.fori_loop(0, 3, rest, 0)
        yield

        def add(x, y):
            return (x.astype(F32) + y.astype(F32)).astype(BF16)

        arrive(s1)
        msg[c, 0, :, low_half] = add(term[c, 1, :, low_half], r1[c, 0])
        msg[c, 0, :, high_half] = term[c, 1, :, high_half]
        s3 = send(msg.at[c, 0], r2.at[c, 0], a_next)
        yield
        arrive(s2)
        msg[c, 1, :, high_half] = add(term[c, 3, :, high_half], r1[c, 1])
        msg[c, 1, :, low_half] = term[c, 3, :, low_half]
        s4 = send(msg.at[c, 1], r2.at[c, 1], a_prev)
        yield
        arrive(s3, s4)

        def total4(k, carry):
            ubuf[c, k] = (term[c, 0, k].astype(F32) + r2[c, 0, k].astype(F32)
                          + r2[c, 1, k].astype(F32)).astype(BF16)
            return carry

        total4(lax.rem(b + 2, 4), 0)
        s5 = send(ubuf.at[c, lax.rem(b + 2, 4), low_half], r3.at[c, 0], b_next)
        s6 = send(ubuf.at[c, lax.rem(b + 2, 4), high_half], r3.at[c, 1], b_prev)
        yield
        total4(lax.rem(b + 1, 4), 0)
        total4(lax.rem(b + 3, 4), 0)
        total4(b, 0)
        yield
        arrive(s5)
        up, down = lax.rem(b + 1, 4), lax.rem(b + 3, 4)
        msg4[c, 0, low_half] = add(ubuf[c, up, low_half], r3[c, 0])
        msg4[c, 0, high_half] = ubuf[c, up, high_half]
        s7 = send(msg4.at[c, 0], r4.at[c, 0], b_next)
        yield
        arrive(s6)
        msg4[c, 1, high_half] = add(ubuf[c, down, high_half], r3[c, 1])
        msg4[c, 1, low_half] = ubuf[c, down, low_half]
        s8 = send(msg4.at[c, 1], r4.at[c, 1], b_prev)
        yield
        arrive(s7, s8)
        fin[c] = (ubuf[c, b].astype(F32) + r4[c, 0].astype(F32) + r4[c, 1].astype(F32)).astype(BF16)
        yield

    streams = {}
    for c in range(2 * NH):
        streams["G%d" % c] = gather(c)
        streams["Q%d" % c] = project(c)
        streams["Z%d" % c] = zring(c)
        streams["R%d" % c] = reduce(c)

    wo_local, wo_remote = [], []
    for i in range(4):
        for k in range(4):
            t = i * sa + k * sb
            cp = pltpu.make_async_copy(
                w_out.at[:, pl.ds(pl.multiple_of(t * W + m * HD, HD), HD)],
                wo.at[i, pl.ds(0, 256), pl.ds(k * HD, HD)], loc_sem.at[NH + 3 + i * 4 + k])
            cp.start()
            wo_local.append(cp)
    for cp in own_copies:
        cp.wait()
    arrive(*swap)
    seen = set()
    for name in ORDER:
        if name[0] == "A":
            attend("LU".index(name[1]), "LU".index(name[2]), int(name[3]))
            continue
        if name[0] == "Q" and "Q" not in seen:
            seen.add("Q")
            o_acc[...] = jnp.zeros_like(o_acc)
            l_acc[...] = jnp.zeros_like(l_acc)
            for cp in w_local:
                cp.wait()
            arrive(*w_remote)
        if name == "Z0" and "Z" not in seen:
            seen.add("Z")
            for i in range(4):
                for k in range(4):
                    t = i * sb + k * sa
                    wo_remote.append(send(
                        w_out.at[:, pl.ds(pl.multiple_of(t * W + sib * HD, HD), HD)],
                        wo.at[i, pl.ds(256, 256), pl.ds(k * HD, HD)], other))
        if name[0] == "R" and "R" not in seen:
            seen.add("R")
            for cp in wo_local:
                cp.wait()
            arrive(*wo_remote)
        next(streams[name])

    back = []
    for h in range(NH):
        back.append(send(fin.at[sib * NH + h], fin_in.at[h], other))
    for h in range(NH):
        arrive(back[h])
        own = fin[m * NH + h]
        got = fin_in[h]
        lower = jnp.full(own.shape, m, jnp.int32) == 0
        out_ref[h * R:(h + 1) * R, 0:HD] = jnp.where(lower, own, got)
        out_ref[h * R:(h + 1) * R, HD:2 * HD] = jnp.where(lower, got, own)
    for cp in sent:
        cp.wait_send()


def body(tokens, modality, norm_gain, input_weight, head_gain, output_weight):
    chunks = 2 * NH
    vmem = pl.BlockSpec(memory_space=pltpu.VMEM)
    anywhere = pl.BlockSpec(memory_space=pl.ANY)
    w3 = jnp.transpose(input_weight[0], (1, 0, 2))
    return pl.pallas_call(
        kernel,
        out_shape=jax.ShapeDtypeStruct((TOK, W), BF16),
        in_specs=[pl.BlockSpec(memory_space=pltpu.SMEM), vmem, vmem, anywhere, vmem, anywhere],
        out_specs=vmem,
        scratch_shapes=[
            pltpu.VMEM((chunks, 16, R, W), BF16),
            pltpu.VMEM((D, 6 * HD), BF16),
            pltpu.VMEM((4, 512, 512), BF16),
            pltpu.VMEM((chunks, R, 6 * HD), F32),
            pltpu.VMEM((chunks, R, 128), F32),
            pltpu.VMEM((2 * TOK, HD), BF16),
            pltpu.VMEM((2, 8, TOK, 2 * HD), BF16),
            pltpu.VMEM((2 * TOK, HD), F32),
            pltpu.VMEM((2 * TOK, 128), F32),
            pltpu.VMEM((chunks, 2, R, HD), BF16),
            pltpu.VMEM((chunks, 4, 4, R, 128), BF16),
            pltpu.VMEM((chunks, R, 512), BF16),
            pltpu.VMEM((chunks, 2, 4, R // 2, 128), BF16),
            pltpu.VMEM((chunks, 2, 4, R, 128), BF16),
            pltpu.VMEM((chunks, 2, 4, R, 128), BF16),
            pltpu.VMEM((chunks, 4, R, 128), BF16),
            pltpu.VMEM((chunks, 2, R // 2, 128), BF16),
            pltpu.VMEM((chunks, 2, R, 128), BF16),
            pltpu.VMEM((chunks, 2, R, 128), BF16),
            pltpu.VMEM((chunks, R, 128), BF16),
            pltpu.VMEM((NH, R, 128), BF16),
            pltpu.SemaphoreType.DMA((N_SEM,)),
            pltpu.SemaphoreType.DMA((N_SEM,)),
            pltpu.SemaphoreType.DMA((NH + 3 + 16,)),
        ],
        compiler_params=pltpu.CompilerParams(
            collective_id=0, has_side_effects=True, vmem_limit_bytes=56 * 1024 * 1024),
    )(modality, tokens, norm_gain, w3, head_gain, output_weight[0])


def solution(mesh):
    in_specs = (
        P(("mod", "seq"), "tp"),
        P(),
        P(),
        P("mod", None, None, "tp"),
        P(),
        P("mod", "tp", None),
    )
    out_specs = P(("mod", "seq"), "tp")
    return jax.shard_map(body, mesh=mesh, in_specs=in_specs, out_specs=out_specs, check_vma=False)
```

time: 136 us -> 113 us (0.83)
  Pallas kernels: 133 us -> 111 us
    pallas_call x1, Pallas kernels: 133 us -> 111 us  [body(): pl.pallas_call(kernel, out_shape=jax.ShapeDtypeStruct((TOK, W), BF16), in...]
where the time goes in v2:
time: 113 us
  Pallas kernels  111 us (98%)
  local copies, waits for them, and re-layouts  1.67 us (1%)
    pallas_call x1, Pallas kernels, body(): pl.pallas_call(kernel, out_shape=jax.ShapeDtypeStruct((TOK, W), BF16), in...  111 us

profile of v2, /device:TPU:1, one launch (start us, length us, event | category | flops | bytes accessed | tf_op | source)
XLA Modules:
  0.0 112.6 jit_solution(6747079711490845762)
XLA Ops:
  0.0 110.9 %shard_map.64 = bf16[512,256]{1,0:T(8,128)(2,1)} custom-call(s32[8192]{0:T(1024)} %mod_ref.1, bf16[512,256]{1,0:T(8,128)(2,1)} %tok_in.1, f32[2,4096]{1,0:T(2,128)} %gain_ref.1, bf16[3,4096,256]{2,1,0:T(8,128)(2,1)} %bitcast.4, f32[2,2,128]{2,1,0:T(2,128)} %hg_ref.1, bf16[256,4096]{1,0:T(8,128)(2,1)} %bitcast.5), custom_call_target="tpu_custom_call" | custom-call | tf_op jit(solution)/shard_map/pallas_call | solution.py:435
  110.9 1.7 %copy.8 = bf16[512,256]{1,0:T(8,128)(2,1)} copy(bf16[512,256]{1,0:T(8,128)(2,1)} %shard_map.64) | data formatting | bytes 524288

commit v3 on v2

--- a/solution.py
+++ b/solution.py
@@ -22,16 +22,15 @@
 Q4 = H // 2
 TQ = 256
 ORDER = (
-    "G0", "G0", "G0", "Q0", "Q1", "Q2", "Q3", "G0", "G0", "G0", "G1", "G0", "Q0", "G0", "Q0", "G0",
-    "G0", "G1", "G1", "G0", "G0", "Q0", "G1", "G1", "G1", "G2", "G1", "Q0", "Q0", "Z0", "Q1", "Q1",
-    "G1", "G1", "G1", "G2", "G2", "G1", "G1", "Z0", "Z0", "Q1", "G2", "G2", "G2", "G2", "G3", "Q1",
-    "Q1", "Z1", "Q2", "Q2", "Z0", "Z0", "G2", "G2", "G2", "G2", "ALL0", "G3", "G3", "G2", "Z1", "Z1",
-    "ALL1", "Q2", "G3", "G3", "G3", "G3", "Q2", "Z0", "Z0", "Q2", "Z2", "Q3", "Q3", "Z1", "Z1", "G3",
-    "G3", "G3", "G3", "ALL2", "G3", "Q3", "Z2", "Z2", "Q3", "Q3", "Z3", "AUU0", "Z1", "Z1", "ALL3", "ALU0",
-    "ALU1", "Z2", "Z2", "ALU2", "ALU3", "Z3", "Z3", "AUU1", "ALL4", "R0", "R1", "ALU4", "R0", "R0", "Z2", "Z2",
-    "R1", "R1", "Z3", "Z3", "AUU2", "R0", "R0", "R1", "R1", "Z3", "Z3", "AUU3", "R0", "R0", "AUU4", "R2",
-    "R3", "R0", "R1", "R0", "R1", "R2", "R2", "R3", "R3", "R0", "R1", "R1", "R2", "R2", "R3", "R3",
-    "R1", "R2", "R2", "R3", "R2", "R3", "R2", "R3", "R3", "R2", "R3",
+    "G0", "G0", "G0", "Q0", "G0", "G0", "G1", "Q3", "Q1", "Q2", "G0", "G0", "G0", "G0", "Q0", "G1",
+    "G1", "Q0", "G0", "G1", "G0", "G1", "G0", "Q0", "G1", "G1", "Q0", "G1", "G1", "G2", "Q0", "Z0",
+    "Q1", "G1", "Q1", "G1", "G1", "G2", "G2", "G3", "Q1", "Z0", "Z0", "G2", "G2", "Q1", "Q1", "Z1",
+    "G2", "ALL0", "G2", "G3", "G3", "Q2", "Z0", "Z0", "G3", "G3", "G2", "G2", "Q2", "G3", "G2", "G2",
+    "Z1", "Z1", "G3", "ALL1", "G3", "G3", "Q3", "Z0", "Z0", "G3", "G2", "G3", "Q3", "Q2", "Z1", "Z1",
+    "G3", "Q2", "Q2", "Z2", "Q3", "Q3", "Q3", "Z3", "AUU0", "Z1", "Z1", "ALL3", "ALL2", "ALU0", "Z2", "Z2",
+    "ALU2", "ALU1", "Z3", "Z3", "AUU1", "ALL4", "R0", "R1", "ALU4", "ALU3", "Z2", "Z2", "R0", "R0", "R1", "R1",
+    "Z3", "Z3", "AUU2", "R0", "R0", "Z2", "Z2", "R1", "R1", "Z3", "Z3", "AUU3", "R0", "AUU4", "R2", "R3",
+    "R2", "R1", "R2", "R3", "R0", "R3", "R2", "R2", "R1", "R3", "R3", "R2", "R3", "R2", "R3",
 )
 QSCALE = math.log2(math.e) / math.sqrt(HD)
 N_SEM = 256
@@ -39,7 +38,7 @@
 
 def kernel(mod_ref, tok_in, gain_ref, w_in, hg_ref, w_out, out_ref,
            tok, wcat, wo, acc, ssq, qbuf, kv, o_acc, l_acc, att, term,
-           abuf, r1, r2, msg, ubuf, r3, msg4, r4, fin, fin_in,
+           abuf, r1, r2, msg, ubuf, r4, fin, fin_in,
            send_sem, recv_sem, loc_sem):
     m = lax.axis_index("mod")
     z = lax.axis_index("seq")
@@ -55,13 +54,14 @@
 
     a_next, a_prev = {"tp": slot(1, 0)}, {"tp": slot(3, 0)}
     b_next, b_prev = {"tp": slot(0, 1)}, {"tp": slot(0, 3)}
+    a_far, b_far = {"tp": slot(2, 0)}, {"tp": slot(0, 2)}
     z_next, z_prev = {"seq": lax.rem(z + 1, 8)}, {"seq": lax.rem(z + 7, 8)}
     other = {"mod": sib}
 
     barrier = pltpu.get_barrier_semaphore()
-    for dev in (a_next, a_prev, b_next, b_prev, z_next, z_prev, other):
+    for dev in (a_next, a_prev, a_far, b_next, b_prev, b_far, z_next, z_prev, other):
         pl.semaphore_signal(barrier, inc=1, device_id=dev, device_id_type=MESH)
-    pl.semaphore_wait(barrier, 7)
+    pl.semaphore_wait(barrier, 9)
 
     sent = []
     count = [0]
@@ -128,24 +128,23 @@
         own = slot(0, 0)
         ar = put(own, rows, a_next)
         al = put(own, rows, a_prev)
+        af = put(own, rows, a_far)
         bn, bp = {}, {}
         d2d = hops[c] = {}
         bn[0] = put(own, rows, b_next)
         bp[0] = put(own, rows, b_prev)
         yield
         arrive(ar)
-        f1 = put(slot(3, 0), low, a_next)
         bn[3] = put(slot(3, 0), rows, b_next)
         bp[3] = put(slot(3, 0), rows, b_prev)
         d2d[3, 0] = put(slot(3, 0), rows, other)
         yield
         arrive(al)
-        f2 = put(slot(1, 0), high, a_prev)
         bn[1] = put(slot(1, 0), rows, b_next)
         bp[1] = put(slot(1, 0), rows, b_prev)
         d2d[1, 0] = put(slot(1, 0), rows, other)
         yield
-        arrive(f1, f2)
+        arrive(af)
         bn[2] = put(slot(2, 0), rows, b_next)
         bp[2] = put(slot(2, 0), rows, b_prev)
         d2d[2, 0] = put(slot(2, 0), rows, other)
@@ -344,27 +343,16 @@
                           + r2[c, 1, k].astype(F32)).astype(BF16)
             return carry
 
-        total4(lax.rem(b + 2, 4), 0)
-        s5 = send(ubuf.at[c, lax.rem(b + 2, 4), low_half], r3.at[c, 0], b_next)
-        s6 = send(ubuf.at[c, lax.rem(b + 2, 4), high_half], r3.at[c, 1], b_prev)
-        yield
-        total4(lax.rem(b + 1, 4), 0)
-        total4(lax.rem(b + 3, 4), 0)
+        reach = []
+        for k, (i, dev) in enumerate(((2, b_far), (1, b_next), (3, b_prev))):
+            to = lax.rem(b + i, 4)
+            total4(to, 0)
+            reach.append(send(ubuf.at[c, to], r4.at[c, k], dev))
         total4(b, 0)
         yield
-        arrive(s5)
-        up, down = lax.rem(b + 1, 4), lax.rem(b + 3, 4)
-        msg4[c, 0, low_half] = add(ubuf[c, up, low_half], r3[c, 0])
-        msg4[c, 0, high_half] = ubuf[c, up, high_half]
-        s7 = send(msg4.at[c, 0], r4.at[c, 0], b_next)
-        yield
-        arrive(s6)
-        msg4[c, 1, high_half] = add(ubuf[c, down, high_half], r3[c, 1])
-        msg4[c, 1, low_half] = ubuf[c, down, low_half]
-        s8 = send(msg4.at[c, 1], r4.at[c, 1], b_prev)
-        yield
-        arrive(s7, s8)
-        fin[c] = (ubuf[c, b].astype(F32) + r4[c, 0].astype(F32) + r4[c, 1].astype(F32)).astype(BF16)
+        arrive(*reach)
+        fin[c] = (ubuf[c, b].astype(F32) + r4[c, 0].astype(F32) + r4[c, 1].astype(F32)
+                  + r4[c, 2].astype(F32)).astype(BF16)
         yield
 
     streams = {}
@@ -454,9 +442,7 @@
             pltpu.VMEM((chunks, 2, 4, R, 128), BF16),
             pltpu.VMEM((chunks, 2, 4, R, 128), BF16),
             pltpu.VMEM((chunks, 4, R, 128), BF16),
-            pltpu.VMEM((chunks, 2, R // 2, 128), BF16),
-            pltpu.VMEM((chunks, 2, R, 128), BF16),
-            pltpu.VMEM((chunks, 2, R, 128), BF16),
+            pltpu.VMEM((chunks, 3, R, 128), BF16),
             pltpu.VMEM((chunks, R, 128), BF16),
             pltpu.VMEM((NH, R, 128), BF16),
             pltpu.SemaphoreType.DMA((N_SEM,)),

time: 113 us -> 107 us (0.947)
  Pallas kernels: 111 us -> 105 us
    pallas_call x1, Pallas kernels: 111 us -> 105 us  [body(): pl.pallas_call(kernel, out_shape=jax.ShapeDtypeStruct((TOK, W), BF16), in...]
where the time goes in v3:
time: 107 us
  Pallas kernels  105 us (98%)
  local copies, waits for them, and re-layouts  1.67 us (2%)
    pallas_call x1, Pallas kernels, body(): pl.pallas_call(kernel, out_shape=jax.ShapeDtypeStruct((TOK, W), BF16), in...  105 us

profile of v3, /device:TPU:1, one launch (start us, length us, event | category | flops | bytes accessed | tf_op | source)
XLA Modules:
  0.0 106.6 jit_solution(9016680222356221920)
XLA Ops:
  0.0 104.9 %shard_map.64 = bf16[512,256]{1,0:T(8,128)(2,1)} custom-call(s32[8192]{0:T(1024)} %mod_ref.1, bf16[512,256]{1,0:T(8,128)(2,1)} %tok_in.1, f32[2,4096]{1,0:T(2,128)} %gain_ref.1, bf16[3,4096,256]{2,1,0:T(8,128)(2,1)} %bitcast.4, f32[2,2,128]{2,1,0:T(2,128)} %hg_ref.1, bf16[256,4096]{1,0:T(8,128)(2,1)} %bitcast.5), custom_call_target="tpu_custom_call" | custom-call | tf_op jit(solution)/shard_map/pallas_call | solution.py:423
  104.9 1.7 %copy.8 = bf16[512,256]{1,0:T(8,128)(2,1)} copy(bf16[512,256]{1,0:T(8,128)(2,1)} %shard_map.64) | data formatting | bytes 524288

commit v4 on v3

--- a/solution.py
+++ b/solution.py
@@ -22,16 +22,18 @@
 Q4 = H // 2
 TQ = 256
 ORDER = (
-    "G0", "G0", "G0", "Q0", "G0", "G0", "G1", "Q3", "Q1", "Q2", "G0", "G0", "G0", "G0", "Q0", "G1",
-    "G1", "Q0", "G0", "G1", "G0", "G1", "G0", "Q0", "G1", "G1", "Q0", "G1", "G1", "G2", "Q0", "Z0",
-    "Q1", "G1", "Q1", "G1", "G1", "G2", "G2", "G3", "Q1", "Z0", "Z0", "G2", "G2", "Q1", "Q1", "Z1",
-    "G2", "ALL0", "G2", "G3", "G3", "Q2", "Z0", "Z0", "G3", "G3", "G2", "G2", "Q2", "G3", "G2", "G2",
-    "Z1", "Z1", "G3", "ALL1", "G3", "G3", "Q3", "Z0", "Z0", "G3", "G2", "G3", "Q3", "Q2", "Z1", "Z1",
-    "G3", "Q2", "Q2", "Z2", "Q3", "Q3", "Q3", "Z3", "AUU0", "Z1", "Z1", "ALL3", "ALL2", "ALU0", "Z2", "Z2",
-    "ALU2", "ALU1", "Z3", "Z3", "AUU1", "ALL4", "R0", "R1", "ALU4", "ALU3", "Z2", "Z2", "R0", "R0", "R1", "R1",
-    "Z3", "Z3", "AUU2", "R0", "R0", "Z2", "Z2", "R1", "R1", "Z3", "Z3", "AUU3", "R0", "AUU4", "R2", "R3",
-    "R2", "R1", "R2", "R3", "R0", "R3", "R2", "R2", "R1", "R3", "R3", "R2", "R3", "R2", "R3",
+    "G0", "G0", "G0", "Q3", "G0", "G0", "G1", "Q2", "Q1", "Q0", "G0", "G0", "G0", "G0", "Q0", "G1",
+    "G1", "Q0", "G1", "G2", "G1", "G0", "G0", "G0", "Q0", "G1", "G1", "Q0", "G1", "Q0", "Z0", "G2",
+    "G2", "Q1", "Q1", "G2", "G2", "G1", "G1", "G1", "G1", "G2", "G3", "Q1", "Z0", "Z0", "G2", "Q1",
+    "G2", "Q1", "Z1", "G2", "Q2", "G2", "G3", "G3", "Q2", "ALL0", "G3", "G2", "G3", "Z0", "Z0", "G2",
+    "Q2", "G3", "G3", "Q2", "Z1", "Z1", "G3", "Q2", "Z2", "G3", "Q3", "Q3", "Z0", "Z0", "G3", "G3",
+    "ALL1", "G3", "Q3", "Z1", "Z1", "Q3", "Q3", "Z3", "AUU0", "ALL2", "Z2", "Z2", "ALU0", "ALU1", "ALU2", "Z1",
+    "Z1", "ALL3", "ALU3", "Z3", "Z3", "AUU1", "Z2", "Z2", "ALL4", "R1", "R0", "ALU4", "R1", "R1", "Z3", "Z3",
+    "R0", "R0", "AUU2", "Z2", "Z2", "R1", "R1", "R0", "R0", "Z3", "Z3", "AUU3", "AUU4", "R3", "R1", "R2",
+    "R3", "R3", "R2", "R2", "R0", "R1", "R3", "R3", "R2", "R2", "R0", "R3", "R2", "R3", "R2",
 )
+LAG = 40
+LAST = 7
 QSCALE = math.log2(math.e) / math.sqrt(HD)
 N_SEM = 256
 
@@ -61,7 +63,30 @@
     barrier = pltpu.get_barrier_semaphore()
     for dev in (a_next, a_prev, a_far, b_next, b_prev, b_far, z_next, z_prev, other):
         pl.semaphore_signal(barrier, inc=1, device_id=dev, device_id_type=MESH)
+    tme = slot(0, 0)
+    own_copies, w_local, wo_local, wo_remote = [], [], [], []
+    for h in range(NH):
+        cp = pltpu.make_async_copy(tok_in.at[pl.ds(h * R, R), :], tok.at[m * NH + h, tme], loc_sem.at[h])
+        cp.start()
+        own_copies.append(cp)
+    for p in range(3):
+        cp = pltpu.make_async_copy(
+            w_in.at[p, :, pl.ds(pl.multiple_of(m * HD, HD), HD)],
+            wcat.at[:, pl.ds(p * HD, HD)], loc_sem.at[NH + p])
+        cp.start()
+        w_local.append(cp)
+    for i in range(4):
+        for k in range(4):
+            t = i * sa + k * sb
+            cp = pltpu.make_async_copy(
+                w_out.at[:, pl.ds(pl.multiple_of(t * W + m * HD, HD), HD)],
+                wo.at[i, pl.ds(0, 256), pl.ds(k * HD, HD)], loc_sem.at[NH + 3 + i * 4 + k])
+            cp.start()
+            wo_local.append(cp)
+    o_acc[...] = jnp.zeros_like(o_acc)
+    l_acc[...] = jnp.zeros_like(l_acc)
     pl.semaphore_wait(barrier, 9)
+
 
     sent = []
     count = [0]
@@ -91,25 +116,11 @@
     def pick(flag, one, zero):
         return jnp.where(jnp.full(one.shape, flag, jnp.int32) == 1, one, zero)
 
-    tme = slot(0, 0)
     swap = []
-    own_copies = []
+    w_remote = []
     for h in range(NH):
-        src = tok_in.at[pl.ds(h * R, R), :]
-        dst = tok.at[m * NH + h, tme]
-        swap.append(send(src, dst, other))
-        cp = pltpu.make_async_copy(src, dst, loc_sem.at[h])
-        cp.start()
-        own_copies.append(cp)
-
-    w_local = []
-    w_remote = []
+        swap.append(send(tok_in.at[pl.ds(h * R, R), :], tok.at[m * NH + h, tme], other))
     for p in range(3):
-        cp = pltpu.make_async_copy(
-            w_in.at[p, :, pl.ds(pl.multiple_of(m * HD, HD), HD)],
-            wcat.at[:, pl.ds(p * HD, HD)], loc_sem.at[NH + p])
-        cp.start()
-        w_local.append(cp)
         w_remote.append(send(
             w_in.at[p, :, pl.ds(pl.multiple_of(sib * HD, HD), HD)],
             wcat.at[:, pl.ds(384 + p * HD, HD)], other))
@@ -163,10 +174,9 @@
             d2d[i, 2] = put(slot(i, 2), rows, other)
             yield
 
-    def unit(c, t):
+    def scaled_slice(c, t):
         x = tok[c, t]
-        first = pl.multiple_of(t * W, W)
-        g = gain_ref[:, pl.ds(first, W)]
+        g = gain_ref[:, pl.ds(pl.multiple_of(t * W, W), W)]
         scaled, squares = [], []
         for k in range(R // SPAN):
             flag = span_mod(c, k)
@@ -174,18 +184,28 @@
             sq = xb * xb
             squares.append(sq[:, :128] + sq[:, 128:])
             scaled.append((xb * pick(flag, g[1:2], g[0:1])).astype(BF16))
-        return (jnp.concatenate(squares, axis=0),
-                jnp.dot(jnp.concatenate(scaled, axis=0), wcat[pl.ds(first, W), :],
-                        preferred_element_type=F32))
+        return jnp.concatenate(squares, axis=0), jnp.concatenate(scaled, axis=0)
+
+    def unit(c, *slots):
+        parts = [scaled_slice(c, t) for t in slots]
+        rows = [wcat[pl.ds(pl.multiple_of(t * W, W), W), :] for t in slots]
+        squares = parts[0][0]
+        for part in parts[1:]:
+            squares = squares + part[0]
+        lhs = jnp.concatenate([part[1] for part in parts], axis=1)
+        return squares, jnp.dot(lhs, jnp.concatenate(rows, axis=0), preferred_element_type=F32)
 
     def units(c, n, where):
-        def step(q, carry):
-            i, k = where(q)
-            squares, part = unit(c, slot(i, k))
+        def two(q, carry):
+            squares, part = unit(c, slot(*where(2 * q)), slot(*where(2 * q + 1)))
             ssq[c] += squares
             acc[c] += part
             return carry
-        lax.fori_loop(0, n, step, 0)
+        lax.fori_loop(0, n // 2, two, 0)
+        if n % 2:
+            squares, part = unit(c, slot(*where(n - 1)))
+            ssq[c] += squares
+            acc[c] += part
 
     def project(c):
         ssq[c], acc[c] = unit(c, slot(0, 0))
@@ -362,27 +382,25 @@
         streams["Z%d" % c] = zring(c)
         streams["R%d" % c] = reduce(c)
 
-    wo_local, wo_remote = [], []
-    for i in range(4):
-        for k in range(4):
-            t = i * sa + k * sb
-            cp = pltpu.make_async_copy(
-                w_out.at[:, pl.ds(pl.multiple_of(t * W + m * HD, HD), HD)],
-                wo.at[i, pl.ds(0, 256), pl.ds(k * HD, HD)], loc_sem.at[NH + 3 + i * 4 + k])
-            cp.start()
-            wo_local.append(cp)
     for cp in own_copies:
         cp.wait()
     arrive(*swap)
     seen = set()
-    for name in ORDER:
+    issued = []
+    turns = {}
+    back = {}
+    retired = 0
+    for number, name in enumerate(ORDER):
+        issued.append(len(sent))
+        if number >= LAG:
+            while retired < issued[number - LAG]:
+                sent[retired].wait_send()
+                retired += 1
         if name[0] == "A":
             attend("LU".index(name[1]), "LU".index(name[2]), int(name[3]))
             continue
         if name[0] == "Q" and "Q" not in seen:
             seen.add("Q")
-            o_acc[...] = jnp.zeros_like(o_acc)
-            l_acc[...] = jnp.zeros_like(l_acc)
             for cp in w_local:
                 cp.wait()
             arrive(*w_remote)
@@ -400,10 +418,12 @@
                 cp.wait()
             arrive(*wo_remote)
         next(streams[name])
-
-    back = []
-    for h in range(NH):
-        back.append(send(fin.at[sib * NH + h], fin_in.at[h], other))
+        if name[0] == "R":
+            turns[name] = turns.get(name, 0) + 1
+            h = int(name[1]) % NH
+            if turns.get("R%d" % h) == LAST and turns.get("R%d" % (h + NH)) == LAST:
+                back[h] = send(fin.at[sib * NH + h], fin_in.at[h], other)
+
     for h in range(NH):
         arrive(back[h])
         own = fin[m * NH + h]
@@ -411,7 +431,7 @@
         lower = jnp.full(own.shape, m, jnp.int32) == 0
         out_ref[h * R:(h + 1) * R, 0:HD] = jnp.where(lower, own, got)
         out_ref[h * R:(h + 1) * R, HD:2 * HD] = jnp.where(lower, got, own)
-    for cp in sent:
+    for cp in sent[retired:]:
         cp.wait_send()
 
 

time: 107 us -> 105 us (0.981)
  Pallas kernels: 105 us -> 103 us
    pallas_call x1, Pallas kernels: 105 us -> 103 us  [body(): pl.pallas_call(kernel, out_shape=jax.ShapeDtypeStruct((TOK, W), BF16), in...]
where the time goes in v4:
time: 105 us
  Pallas kernels  103 us (98%)
  local copies, waits for them, and re-layouts  1.67 us (2%)
    pallas_call x1, Pallas kernels, body(): pl.pallas_call(kernel, out_shape=jax.ShapeDtypeStruct((TOK, W), BF16), in...  103 us

profile of v4, /device:TPU:1, one launch (start us, length us, event | category | flops | bytes accessed | tf_op | source)
XLA Modules:
  0.0 104.7 jit_solution(6024213902354818297)
XLA Ops:
  0.0 103.0 %shard_map.64 = bf16[512,256]{1,0:T(8,128)(2,1)} custom-call(s32[8192]{0:T(1024)} %mod_ref.1, bf16[512,256]{1,0:T(8,128)(2,1)} %tok_in.1, f32[2,4096]{1,0:T(2,128)} %gain_ref.1, bf16[3,4096,256]{2,1,0:T(8,128)(2,1)} %bitcast.4, f32[2,2,128]{2,1,0:T(2,128)} %hg_ref.1, bf16[256,4096]{1,0:T(8,128)(2,1)} %bitcast.5), custom_call_target="tpu_custom_call" | custom-call | tf_op jit(solution)/shard_map/pallas_call | solution.py:443
  103.0 1.7 %copy.8 = bf16[512,256]{1,0:T(8,128)(2,1)} copy(bf16[512,256]{1,0:T(8,128)(2,1)} %shard_map.64) | data formatting | bytes 524288

commit v5 on v4

--- a/solution.py
+++ b/solution.py
@@ -22,15 +22,15 @@
 Q4 = H // 2
 TQ = 256
 ORDER = (
-    "G0", "G0", "G0", "Q3", "G0", "G0", "G1", "Q2", "Q1", "Q0", "G0", "G0", "G0", "G0", "Q0", "G1",
-    "G1", "Q0", "G1", "G2", "G1", "G0", "G0", "G0", "Q0", "G1", "G1", "Q0", "G1", "Q0", "Z0", "G2",
-    "G2", "Q1", "Q1", "G2", "G2", "G1", "G1", "G1", "G1", "G2", "G3", "Q1", "Z0", "Z0", "G2", "Q1",
-    "G2", "Q1", "Z1", "G2", "Q2", "G2", "G3", "G3", "Q2", "ALL0", "G3", "G2", "G3", "Z0", "Z0", "G2",
-    "Q2", "G3", "G3", "Q2", "Z1", "Z1", "G3", "Q2", "Z2", "G3", "Q3", "Q3", "Z0", "Z0", "G3", "G3",
-    "ALL1", "G3", "Q3", "Z1", "Z1", "Q3", "Q3", "Z3", "AUU0", "ALL2", "Z2", "Z2", "ALU0", "ALU1", "ALU2", "Z1",
-    "Z1", "ALL3", "ALU3", "Z3", "Z3", "AUU1", "Z2", "Z2", "ALL4", "R1", "R0", "ALU4", "R1", "R1", "Z3", "Z3",
-    "R0", "R0", "AUU2", "Z2", "Z2", "R1", "R1", "R0", "R0", "Z3", "Z3", "AUU3", "AUU4", "R3", "R1", "R2",
-    "R3", "R3", "R2", "R2", "R0", "R1", "R3", "R3", "R2", "R2", "R0", "R3", "R2", "R3", "R2",
+    "G0", "G0", "G0", "Q0", "G0", "G0", "G1", "Q2", "Q3", "Q1", "G0", "G0", "G0", "G0", "Q0", "Q0",
+    "G1", "G1", "G1", "G1", "G2", "G0", "G0", "G0", "Q0", "Q0", "Q0", "Z0", "G1", "G1", "G1", "G1",
+    "Q1", "G2", "G2", "Q1", "G2", "G2", "G1", "G1", "G1", "Z0", "Z0", "Q1", "G2", "Q1", "G2", "G3",
+    "Q1", "Z1", "G2", "G2", "ALL0", "Q2", "G2", "Q2", "Z0", "Z0", "G2", "G3", "G3", "G3", "G3", "G2",
+    "Z1", "Z1", "ALL1", "G3", "Q2", "G3", "G3", "Z0", "Z0", "G3", "Q2", "Q2", "Z2", "Q3", "G3", "Q3",
+    "Z1", "Z1", "G3", "G3", "ALL2", "Q3", "Q3", "Q3", "Z3", "Z2", "Z2", "ALU2", "ALU0", "ALU1", "Z1", "Z1",
+    "ALL3", "ALU3", "Z3", "Z3", "AUU1", "AUU0", "Z2", "Z2", "ALL4", "R0", "R1", "ALU4", "R0", "R0", "Z3", "Z3",
+    "R1", "R1", "AUU2", "Z2", "Z2", "R0", "R0", "R1", "R1", "Z3", "Z3", "AUU3", "AUU4", "R0", "R2", "R3",
+    "R2", "R2", "R3", "R3", "R0", "R1", "R2", "R2", "R3", "R3", "R1", "R2", "R3", "R2", "R3",
 )
 LAG = 40
 LAST = 7

time: 105 us -> 101 us (0.962)
  Pallas kernels: 103 us -> 99.6 us
    pallas_call x1, Pallas kernels: 103 us -> 99.6 us  [body(): pl.pallas_call(kernel, out_shape=jax.ShapeDtypeStruct((TOK, W), BF16), in...]
where the time goes in v5:
time: 101 us
  Pallas kernels  99.6 us (99%)
  local copies, waits for them, and re-layouts  1.67 us (2%)
    pallas_call x1, Pallas kernels, body(): pl.pallas_call(kernel, out_shape=jax.ShapeDtypeStruct((TOK, W), BF16), in...  99.6 us

profile of v5, /device:TPU:1, one launch (start us, length us, event | category | flops | bytes accessed | tf_op | source)
XLA Modules:
  0.0 101.3 jit_solution(944010701293356838)
XLA Ops:
  0.0 99.6 %shard_map.64 = bf16[512,256]{1,0:T(8,128)(2,1)} custom-call(s32[8192]{0:T(1024)} %mod_ref.1, bf16[512,256]{1,0:T(8,128)(2,1)} %tok_in.1, f32[2,4096]{1,0:T(2,128)} %gain_ref.1, bf16[3,4096,256]{2,1,0:T(8,128)(2,1)} %bitcast.4, f32[2,2,128]{2,1,0:T(2,128)} %hg_ref.1, bf16[256,4096]{1,0:T(8,128)(2,1)} %bitcast.5), custom_call_target="tpu_custom_call" | custom-call | tf_op jit(solution)/shard_map/pallas_call | solution.py:443
  99.6 1.7 %copy.8 = bf16[512,256]{1,0:T(8,128)(2,1)} copy(bf16[512,256]{1,0:T(8,128)(2,1)} %shard_map.64) | data formatting | bytes 524288

commit v6 on v5

--- a/solution.py
+++ b/solution.py
@@ -382,9 +382,6 @@
         streams["Z%d" % c] = zring(c)
         streams["R%d" % c] = reduce(c)
 
-    for cp in own_copies:
-        cp.wait()
-    arrive(*swap)
     seen = set()
     issued = []
     turns = {}
@@ -399,6 +396,11 @@
         if name[0] == "A":
             attend("LU".index(name[1]), "LU".index(name[2]), int(name[3]))
             continue
+        if name[0] in "GQ" and ("own", int(name[1]) % NH) not in seen:
+            h = int(name[1]) % NH
+            seen.add(("own", h))
+            own_copies[h].wait()
+            arrive(swap[h])
         if name[0] == "Q" and "Q" not in seen:
             seen.add("Q")
             for cp in w_local:

time: 101 us -> 101 us (level)
  no operation moved by 1% of the time
where the time goes in v6:
time: 101 us
  Pallas kernels  99.3 us (98%)
  local copies, waits for them, and re-layouts  1.67 us (2%)
    pallas_call x1, Pallas kernels, body(): pl.pallas_call(kernel, out_shape=jax.ShapeDtypeStruct((TOK, W), BF16), in...  99.3 us

profile of v6, /device:TPU:1, one launch (start us, length us, event | category | flops | bytes accessed | tf_op | source)
XLA Modules:
  0.0 101.0 jit_solution(11054929593865712168)
XLA Ops:
  0.0 99.3 %shard_map.64 = bf16[512,256]{1,0:T(8,128)(2,1)} custom-call(s32[8192]{0:T(1024)} %mod_ref.1, bf16[512,256]{1,0:T(8,128)(2,1)} %tok_in.1, f32[2,4096]{1,0:T(2,128)} %gain_ref.1, bf16[3,4096,256]{2,1,0:T(8,128)(2,1)} %bitcast.4, f32[2,2,128]{2,1,0:T(2,128)} %hg_ref.1, bf16[256,4096]{1,0:T(8,128)(2,1)} %bitcast.5), custom_call_target="tpu_custom_call" | custom-call | tf_op jit(solution)/shard_map/pallas_call | solution.py:445
  99.3 1.7 %copy.8 = bf16[512,256]{1,0:T(8,128)(2,1)} copy(bf16[512,256]{1,0:T(8,128)(2,1)} %shard_map.64) | data formatting | bytes 524288
